TPU v7x, 256 devices: a whole 4x4x8 slice. The times are simulated.
256 devices in a mesh: users: 16 (over x, y), ctx: 16 (over z, core).
Axes of the slice: x: 4, y: 4, z: 8, core: 2. Of those that a mesh axis runs over, the one named last changes fastest.
Arguments:
- cand_feat: bfloat16 [98304, 1024], P(('users', 'ctx')), may hold values from -27 to 27
- cand_user: int32 [98304, 1], P(('users', 'ctx')), may hold values from 0 to 15; in each aligned block of 384 rows (0 to 383, 384 to 767, ...) at most 48 rows name the same one
- hist_kv: bfloat16 [1, 16, 2048, 2048], P(None, 'users', 'ctx'), may hold values from -27 to 27
- hist_mask: int32 [16, 16], P('users'), may hold values from 0 to 1, as said below
- gain_in: float32 [1, 1024], replicated, may hold values from 0.25 to 1.75
- w_uq: bfloat16 [1, 1024, 2048], replicated, may hold values from -0.1875 to 0.1875
- gain_attn: float32 [1, 1024], replicated, may hold values from 0.25 to 1.75
- w_out: bfloat16 [1, 1024, 1024], replicated, may hold values from -0.1875 to 0.1875
Outputs:
- cand_out: bfloat16 [98304, 1024], P(('users', 'ctx'))
Inputs may be any that keep to these rules, and one draw needn't show every extreme that they name: `cand_user`: within the rows of one device no user is named by more than 48 rows, a bound that some block reaches of them. `hist_mask`: every user has exactly 8 ones among its 16 blocks.
All inputs are finite; a program needn't handle non-finite values.
Results may differ from a plain program's by a relative error of at most 0.0039.
Values may be sent and summed in bfloat16 or wider, within the bound.
A program may use at most 128 MiB of HBM per device.

v0:
```python
import jax
import jax.numpy as jnp
from jax import lax
from jax.sharding import PartitionSpec as P

H = 8
BLK = 128


def centred_norm(inputs):
    middle = jnp.mean(inputs, axis=-1, keepdims=True)
    shifted = inputs - middle
    spread = jnp.mean(shifted * shifted, axis=-1, keepdims=True)
    return shifted * lax.rsqrt(spread + 1e-05)


def score_block(running, query_heads, kv_block):
    head_count = query_heads.shape[1]
    head_size = query_heads.shape[2]
    feat_width = head_count * head_size
    key_count = kv_block.shape[0]
    key_heads = kv_block[:, :feat_width].reshape(key_count, head_count, head_size)
    value_heads = kv_block[:, feat_width:].reshape(key_count, head_count, head_size)
    scores = jnp.einsum(
        "shd,khd->hsk", query_heads, key_heads, preferred_element_type=jnp.float32
    ) * head_size ** (-0.5)
    attn_weights = jax.nn.silu(scores).astype(jnp.bfloat16)
    combined = jnp.einsum(
        "hsk,khd->shd", attn_weights, value_heads, preferred_element_type=jnp.float32
    )
    return running + combined.reshape(running.shape)


def on_device(cand_feat, cand_user, hist_kv, hist_mask, gain_in, w_uq, gain_attn, w_out):
    owner_count = lax.axis_size("users")
    row_count, feat_width = cand_feat.shape
    slot_cap = 2 * row_count // owner_count
    slot_rows = owner_count * slot_cap
    target_user = cand_user[:, 0]
    one_hot = (target_user[:, None] == jnp.arange(owner_count, dtype=jnp.int32)[None, :]).astype(
        jnp.int32
    )
    earlier = jnp.cumsum(one_hot, axis=0) - one_hot
    send_slot = target_user * slot_cap + jnp.sum(earlier * one_hot, axis=1)
    outgoing = jnp.zeros((slot_rows, feat_width), jnp.bfloat16).at[send_slot].set(cand_feat)
    arrived = lax.all_to_all(
        outgoing.reshape(owner_count, slot_cap, feat_width),
        "users",
        split_axis=0,
        concat_axis=0,
        tiled=True,
    )
    hidden = arrived.reshape(slot_rows, feat_width)
    block_mask = hist_mask[0]
    block_count = block_mask.shape[0]
    block_range = jnp.arange(block_count, dtype=jnp.int32)
    residual = hidden.astype(jnp.float32)
    normed = (centred_norm(residual) * gain_in[0]).astype(jnp.bfloat16)
    projected = jnp.dot(normed, w_uq[0], preferred_element_type=jnp.float32)
    gate_vals = jax.nn.silu(projected[:, :feat_width])
    queries = jax.nn.silu(projected[:, feat_width:]).astype(jnp.bfloat16)
    query_heads = queries.reshape(slot_rows, H, feat_width // H)
    local_kv = hist_kv[0, 0]
    zero_sum = jnp.zeros((slot_rows, feat_width), jnp.float32)
    shard_rows = lax.all_gather(local_kv, "ctx", axis=0, tiled=True)
    piece_blocks = shard_rows.shape[0] // BLK
    key_blocks = shard_rows.reshape(piece_blocks, BLK, shard_rows.shape[1])
    block_ids = jnp.arange(piece_blocks, dtype=jnp.int32)

    def walk_block(carried, packed):
        block_keys, block_id = packed
        is_live = jnp.sum(jnp.where(block_range == block_id, block_mask, 0))
        updated = lax.cond(
            is_live > 0,
            lambda total: score_block(total, query_heads, block_keys),
            lambda total: total,
            carried,
        )
        return (updated, None)

    result, unused = lax.scan(walk_block, zero_sum, (key_blocks, block_ids))
    mixed = (centred_norm(result) * gain_attn[0] * gate_vals).astype(jnp.bfloat16)
    hidden = (residual + jnp.dot(mixed, w_out[0], preferred_element_type=jnp.float32)).astype(
        jnp.bfloat16
    )
    returned = lax.all_to_all(
        hidden.reshape(owner_count, slot_cap, feat_width),
        "users",
        split_axis=0,
        concat_axis=0,
        tiled=True,
    )
    return returned.reshape(slot_rows, feat_width)[send_slot]


def solution(mesh):
    in_specs = (
        P(("users", "ctx"), None),
        P(("users", "ctx"), None),
        P(None, "users", "ctx", None),
        P("users", None),
        P(),
        P(),
        P(),
        P(),
    )
    out_specs = P(("users", "ctx"), None)
    return jax.shard_map(
        on_device, mesh=mesh, in_specs=in_specs, out_specs=out_specs, check_vma=False
    )
```

profile of v0, /device:TPU:1, one launch (start us, length us, event | category | flops | bytes accessed | tf_op | source)
XLA Modules:
  0.0 269.2 jit_solution(5160739637191431380)
XLA Ops:
  13.9 7.8 %all-to-all-start = ((bf16[16,48,1024]{2,1,0:T(8,128)(2,1)}), bf16[16,48,1024]{2,1,0:T(8,128)(2,1)}, u32[]{:S(2)}, u32[]{:S(2)}) async-start(bf16[16,48,1024]{2,1,0:T(8,128)(2,1)} %bitcast.79), calls=%async_computation | async-start | bytes 3145728 | tf_op jit(solution)/shard_map/all_to_all | solution.py:46
  21.7 20.7 %all-to-all-done = bf16[16,48,1024]{2,1,0:T(8,128)(2,1)} async-done(((bf16[16,48,1024]{2,1,0:T(8,128)(2,1)}), bf16[16,48,1024]{2,1,0:T(8,128)(2,1)}, u32[]{:S(2)}, u32[]{:S(2)}) %all-to-all-start) | async-done | bytes 1572896 | tf_op jit(solution)/shard_map/all_to_all | solution.py:46
  56.4 13.0 %all-gather.3.cloned.1.call-done = bf16[1,1,2048,2048]{3,2,1,0:T(8,128)(2,1)} async-done(((bf16[1,1,128,2048]{3,2,1,0:T(8,128)(2,1)}), bf16[1,1,2048,2048]{3,2,1,0:T(8,128)(2,1)}) %all-gather.3.cloned.1.call-update) | async-done | bytes 8388624 | tf_op jit(solution)/shard_map/all_gather | solution.py:65
  69.3 12.3 %copy.15 = bf16[16,128,2048]{1,2,0:T(8,128)(2,1)} copy(bf16[16,128,2048]{2,1,0:T(8,128)(2,1)} %bitcast.76) | data formatting | bytes 16777216
  83.6 130.1 %while.15 = (s32[]{:T(128)}, f32[768,1024]{0,1:T(8,128)}, s32[16]{0:T(128)S(1)}, s32[16]{0:T(128)S(1)}, bf16[16,128,2048]{1,2,0:T(8,128)(2,1)}, /*index=5*/bf16[768,8,128]{2,0,1:T(8,128)(2,1)}, s32[]{:T(128)}, s32[]{:T(128)}) while((s32[]{:T(128)}, f32[768,1024]{0,1:T(8,128)}, s32[16]{0:T(128)S(1)}, s32[16]{0:T(128)S(1)}, ...), condition=%wide.region_10.11_spmd.clone, body=%wide.region_6.10_spmd.clone.sunk | while | flops 408158272 | bytes 16777508 | solution.py:81
  86.3 10.8 %conditional.3 = (f32[768,1024]{0,1:T(8,128)}) conditional(s32[]{:T(128)} %convert_element_type.73, f32[768,1024]{0,1:T(8,128)} %get-tuple-element.175, (bf16[16,128,2048]{1,2,0:T(8,128)(2,1)}, s32[]{:T(128)}, bf16[768,8,128]{2,0,1:T(8,128)(2,1)}, f32[768,1024]{0,1:T(8,128)}) %tuple.38), branch_computations={%region_8.8_spmd, %region_9.9_spmd} | conditional | flops 408158208 | bytes 16777228 | solution.py:73
  87.4 4.7 %fusion.4 = f32[8,768,128]{1,2,0:T(8,128)} fusion(bf16[128,8,128]{0,2,1:T(8,128)(2,1)S(1)} %bitcast.78, bf16[128,8,128]{0,2,1:T(8,128)(2,1)S(1)} %bitcast.77, bf16[768,8,128]{2,0,1:T(8,128)(2,1)} %get-tuple-element.76), kind=kOutput, calls=%fused_computation.9 | convolution fusion | flops 407371776 | bytes 5242880 | tf_op jit(solution)/shard_map/while/body/eval_jaxpr/cond/branch_1_fun/hsk,khd->shd/dot_general | solution.py:28
  92.1 5.0 %bitcast_add_fusion = f32[768,1024]{0,1:T(8,128)} fusion(f32[768,1024]{0,1:T(8,128)} %get-tuple-element.73, f32[8,768,128]{1,2,0:T(8,128)} %fusion.4), kind=kLoop, calls=%fused_computation.2 | loop fusion | flops 786432 | bytes 9437184 | tf_op jit(solution)/shard_map/while/body/eval_jaxpr/cond/branch_1_fun/add | solution.py:31
  99.8 10.8 %conditional.3 = (f32[768,1024]{0,1:T(8,128)}) conditional(s32[]{:T(128)} %convert_element_type.73, f32[768,1024]{0,1:T(8,128)} %get-tuple-element.175, (bf16[16,128,2048]{1,2,0:T(8,128)(2,1)}, s32[]{:T(128)}, bf16[768,8,128]{2,0,1:T(8,128)(2,1)}, f32[768,1024]{0,1:T(8,128)}) %tuple.38), branch_computations={%region_8.8_spmd, %region_9.9_spmd} | conditional | flops 408158208 | bytes 16777228 | solution.py:73
  100.9 4.7 %fusion.4 = f32[8,768,128]{1,2,0:T(8,128)} fusion(bf16[128,8,128]{0,2,1:T(8,128)(2,1)S(1)} %bitcast.78, bf16[128,8,128]{0,2,1:T(8,128)(2,1)S(1)} %bitcast.77, bf16[768,8,128]{2,0,1:T(8,128)(2,1)} %get-tuple-element.76), kind=kOutput, calls=%fused_computation.9 | convolution fusion | flops 407371776 | bytes 5242880 | tf_op jit(solution)/shard_map/while/body/eval_jaxpr/cond/branch_1_fun/hsk,khd->shd/dot_general | solution.py:28
  105.7 5.0 %bitcast_add_fusion = f32[768,1024]{0,1:T(8,128)} fusion(f32[768,1024]{0,1:T(8,128)} %get-tuple-element.73, f32[8,768,128]{1,2,0:T(8,128)} %fusion.4), kind=kLoop, calls=%fused_computation.2 | loop fusion | flops 786432 | bytes 9437184 | tf_op jit(solution)/shard_map/while/body/eval_jaxpr/cond/branch_1_fun/add | solution.py:31
  116.1 10.8 %conditional.3 = (f32[768,1024]{0,1:T(8,128)}) conditional(s32[]{:T(128)} %convert_element_type.73, f32[768,1024]{0,1:T(8,128)} %get-tuple-element.175, (bf16[16,128,2048]{1,2,0:T(8,128)(2,1)}, s32[]{:T(128)}, bf16[768,8,128]{2,0,1:T(8,128)(2,1)}, f32[768,1024]{0,1:T(8,128)}) %tuple.38), branch_computations={%region_8.8_spmd, %region_9.9_spmd} | conditional | flops 408158208 | bytes 16777228 | solution.py:73
  117.2 4.7 %fusion.4 = f32[8,768,128]{1,2,0:T(8,128)} fusion(bf16[128,8,128]{0,2,1:T(8,128)(2,1)S(1)} %bitcast.78, bf16[128,8,128]{0,2,1:T(8,128)(2,1)S(1)} %bitcast.77, bf16[768,8,128]{2,0,1:T(8,128)(2,1)} %get-tuple-element.76), kind=kOutput, calls=%fused_computation.9 | convolution fusion | flops 407371776 | bytes 5242880 | tf_op jit(solution)/shard_map/while/body/eval_jaxpr/cond/branch_1_fun/hsk,khd->shd/dot_general | solution.py:28
  121.9 5.0 %bitcast_add_fusion = f32[768,1024]{0,1:T(8,128)} fusion(f32[768,1024]{0,1:T(8,128)} %get-tuple-element.73, f32[8,768,128]{1,2,0:T(8,128)} %fusion.4), kind=kLoop, calls=%fused_computation.2 | loop fusion | flops 786432 | bytes 9437184 | tf_op jit(solution)/shard_map/while/body/eval_jaxpr/cond/branch_1_fun/add | solution.py:31
  129.6 10.8 %conditional.3 = (f32[768,1024]{0,1:T(8,128)}) conditional(s32[]{:T(128)} %convert_element_type.73, f32[768,1024]{0,1:T(8,128)} %get-tuple-element.175, (bf16[16,128,2048]{1,2,0:T(8,128)(2,1)}, s32[]{:T(128)}, bf16[768,8,128]{2,0,1:T(8,128)(2,1)}, f32[768,1024]{0,1:T(8,128)}) %tuple.38), branch_computations={%region_8.8_spmd, %region_9.9_spmd} | conditional | flops 408158208 | bytes 16777228 | solution.py:73
  130.8 4.7 %fusion.4 = f32[8,768,128]{1,2,0:T(8,128)} fusion(bf16[128,8,128]{0,2,1:T(8,128)(2,1)S(1)} %bitcast.78, bf16[128,8,128]{0,2,1:T(8,128)(2,1)S(1)} %bitcast.77, bf16[768,8,128]{2,0,1:T(8,128)(2,1)} %get-tuple-element.76), kind=kOutput, calls=%fused_computation.9 | convolution fusion | flops 407371776 | bytes 5242880 | tf_op jit(solution)/shard_map/while/body/eval_jaxpr/cond/branch_1_fun/hsk,khd->shd/dot_general | solution.py:28
  135.5 5.0 %bitcast_add_fusion = f32[768,1024]{0,1:T(8,128)} fusion(f32[768,1024]{0,1:T(8,128)} %get-tuple-element.73, f32[8,768,128]{1,2,0:T(8,128)} %fusion.4), kind=kLoop, calls=%fused_computation.2 | loop fusion | flops 786432 | bytes 9437184 | tf_op jit(solution)/shard_map/while/body/eval_jaxpr/cond/branch_1_fun/add | solution.py:31
  145.9 10.8 %conditional.3 = (f32[768,1024]{0,1:T(8,128)}) conditional(s32[]{:T(128)} %convert_element_type.73, f32[768,1024]{0,1:T(8,128)} %get-tuple-element.175, (bf16[16,128,2048]{1,2,0:T(8,128)(2,1)}, s32[]{:T(128)}, bf16[768,8,128]{2,0,1:T(8,128)(2,1)}, f32[768,1024]{0,1:T(8,128)}) %tuple.38), branch_computations={%region_8.8_spmd, %region_9.9_spmd} | conditional | flops 408158208 | bytes 16777228 | solution.py:73
  147.0 4.7 %fusion.4 = f32[8,768,128]{1,2,0:T(8,128)} fusion(bf16[128,8,128]{0,2,1:T(8,128)(2,1)S(1)} %bitcast.78, bf16[128,8,128]{0,2,1:T(8,128)(2,1)S(1)} %bitcast.77, bf16[768,8,128]{2,0,1:T(8,128)(2,1)} %get-tuple-element.76), kind=kOutput, calls=%fused_computation.9 | convolution fusion | flops 407371776 | bytes 5242880 | tf_op jit(solution)/shard_map/while/body/eval_jaxpr/cond/branch_1_fun/hsk,khd->shd/dot_general | solution.py:28
  151.7 5.0 %bitcast_add_fusion = f32[768,1024]{0,1:T(8,128)} fusion(f32[768,1024]{0,1:T(8,128)} %get-tuple-element.73, f32[8,768,128]{1,2,0:T(8,128)} %fusion.4), kind=kLoop, calls=%fused_computation.2 | loop fusion | flops 786432 | bytes 9437184 | tf_op jit(solution)/shard_map/while/body/eval_jaxpr/cond/branch_1_fun/add | solution.py:31
  159.4 10.8 %conditional.3 = (f32[768,1024]{0,1:T(8,128)}) conditional(s32[]{:T(128)} %convert_element_type.73, f32[768,1024]{0,1:T(8,128)} %get-tuple-element.175, (bf16[16,128,2048]{1,2,0:T(8,128)(2,1)}, s32[]{:T(128)}, bf16[768,8,128]{2,0,1:T(8,128)(2,1)}, f32[768,1024]{0,1:T(8,128)}) %tuple.38), branch_computations={%region_8.8_spmd, %region_9.9_spmd} | conditional | flops 408158208 | bytes 16777228 | solution.py:73
  165.3 5.0 %bitcast_add_fusion = f32[768,1024]{0,1:T(8,128)} fusion(f32[768,1024]{0,1:T(8,128)} %get-tuple-element.73, f32[8,768,128]{1,2,0:T(8,128)} %fusion.4), kind=kLoop, calls=%fused_computation.2 | loop fusion | flops 786432 | bytes 9437184 | tf_op jit(solution)/shard_map/while/body/eval_jaxpr/cond/branch_1_fun/add | solution.py:31
  181.1 10.8 %conditional.3 = (f32[768,1024]{0,1:T(8,128)}) conditional(s32[]{:T(128)} %convert_element_type.73, f32[768,1024]{0,1:T(8,128)} %get-tuple-element.175, (bf16[16,128,2048]{1,2,0:T(8,128)(2,1)}, s32[]{:T(128)}, bf16[768,8,128]{2,0,1:T(8,128)(2,1)}, f32[768,1024]{0,1:T(8,128)}) %tuple.38), branch_computations={%region_8.8_spmd, %region_9.9_spmd} | conditional | flops 408158208 | bytes 16777228 | solution.py:73
  182.3 4.7 %fusion.4 = f32[8,768,128]{1,2,0:T(8,128)} fusion(bf16[128,8,128]{0,2,1:T(8,128)(2,1)S(1)} %bitcast.78, bf16[128,8,128]{0,2,1:T(8,128)(2,1)S(1)} %bitcast.77, bf16[768,8,128]{2,0,1:T(8,128)(2,1)} %get-tuple-element.76), kind=kOutput, calls=%fused_computation.9 | convolution fusion | flops 407371776 | bytes 5242880 | tf_op jit(solution)/shard_map/while/body/eval_jaxpr/cond/branch_1_fun/hsk,khd->shd/dot_general | solution.py:28
  187.0 5.0 %bitcast_add_fusion = f32[768,1024]{0,1:T(8,128)} fusion(f32[768,1024]{0,1:T(8,128)} %get-tuple-element.73, f32[8,768,128]{1,2,0:T(8,128)} %fusion.4), kind=kLoop, calls=%fused_computation.2 | loop fusion | flops 786432 | bytes 9437184 | tf_op jit(solution)/shard_map/while/body/eval_jaxpr/cond/branch_1_fun/add | solution.py:31
  197.4 10.8 %conditional.3 = (f32[768,1024]{0,1:T(8,128)}) conditional(s32[]{:T(128)} %convert_element_type.73, f32[768,1024]{0,1:T(8,128)} %get-tuple-element.175, (bf16[16,128,2048]{1,2,0:T(8,128)(2,1)}, s32[]{:T(128)}, bf16[768,8,128]{2,0,1:T(8,128)(2,1)}, f32[768,1024]{0,1:T(8,128)}) %tuple.38), branch_computations={%region_8.8_spmd, %region_9.9_spmd} | conditional | flops 408158208 | bytes 16777228 | solution.py:73
  198.6 4.7 %fusion.4 = f32[8,768,128]{1,2,0:T(8,128)} fusion(bf16[128,8,128]{0,2,1:T(8,128)(2,1)S(1)} %bitcast.78, bf16[128,8,128]{0,2,1:T(8,128)(2,1)S(1)} %bitcast.77, bf16[768,8,128]{2,0,1:T(8,128)(2,1)} %get-tuple-element.76), kind=kOutput, calls=%fused_computation.9 | convolution fusion | flops 407371776 | bytes 5242880 | tf_op jit(solution)/shard_map/while/body/eval_jaxpr/cond/branch_1_fun/hsk,khd->shd/dot_general | solution.py:28
  203.3 5.0 %bitcast_add_fusion = f32[768,1024]{0,1:T(8,128)} fusion(f32[768,1024]{0,1:T(8,128)} %get-tuple-element.73, f32[8,768,128]{1,2,0:T(8,128)} %fusion.4), kind=kLoop, calls=%fused_computation.2 | loop fusion | flops 786432 | bytes 9437184 | tf_op jit(solution)/shard_map/while/body/eval_jaxpr/cond/branch_1_fun/add | solution.py:31
  222.2 5.6 %fusion.12 = bf16[768,1024]{1,0:T(8,128)(2,1)} fusion(bf16[16,48,1024]{2,1,0:T(8,128)(2,1)} %all-to-all-done, bf16[1,1024,1024]{2,1,0:T(8,128)(2,1)S(1)} %copy-done, f32[768,2048]{1,0:T(8,128)} %copy-done.2, f32[768,1024]{1,0:T(8,128)S(1)} %copy-done.1, f32[1024]{0:T(1024)S(1)} %bitcast.86, f32[768]{0:T(1024)S(1)} %add_rsqrt_fusion.1, ...), kind=kOutput, calls=%fused_computation.20 | convolution fusion | flops 1620049920 | bytes 11544576 | tf_op jit(solution)/shard_map/dot_general | solution.py:83
  227.9 6.6 %all-to-all-start.1 = ((bf16[16,48,1024]{2,1,0:T(8,128)(2,1)}), bf16[16,48,1024]{2,1,0:T(8,128)(2,1)}, u32[]{:S(2)}, u32[]{:S(2)}) async-start(bf16[16,48,1024]{2,1,0:T(8,128)(2,1)} %bitcast.80), calls=%async_computation.1 | async-start | bytes 3145728 | tf_op jit(solution)/shard_map/all_to_all | solution.py:86
  234.5 22.9 %all-to-all-done.1 = bf16[16,48,1024]{2,1,0:T(8,128)(2,1)} async-done(((bf16[16,48,1024]{2,1,0:T(8,128)(2,1)}), bf16[16,48,1024]{2,1,0:T(8,128)(2,1)}, u32[]{:S(2)}, u32[]{:S(2)}) %all-to-all-start.1) | async-done | bytes 1572896 | tf_op jit(solution)/shard_map/all_to_all | solution.py:86
  257.3 5.0 %gather_fusion = bf16[384,1024]{1,0:T(8,128)(2,1)} fusion(bf16[768,1024]{1,0:T(8,128)(2,1)} %bitcast.17, s32[1024]{0:T(1024)S(1)} %pad_clamp_fusion), kind=kCustom, calls=%fused_computation | custom fusion | bytes 1574400 | tf_op jit(solution)/shard_map/gather | solution.py:93
  (96 shorter events, 77.4 us)
Async XLA Ops:
  6.5 215.4 %copy-start = (bf16[1,1024,1024]{2,1,0:T(8,128)(2,1)S(1)}, bf16[1,1024,1024]{2,1,0:T(8,128)(2,1)}, u32[]{:S(2)}) copy-start(bf16[1,1024,1024]{2,1,0:T(8,128)(2,1)} %param.19) | copy-start | bytes 6291460
  6.5 62.8 %all-gather.3.cloned.1.call-start = ((), (), s32[]{:S(2)}) async-start(), calls=%async_computation.2 | async-start | bytes 8912896 | tf_op jit(solution)/shard_map/all_gather | solution.py:65
  13.9 32.3 %copy-start.4 = (f32[1,1024]{1,0:T(1,128)S(1)}, f32[1,1024]{1,0:T(1,128)}, u32[]{:S(2)}) copy-start(f32[1,1024]{1,0:T(1,128)} %param.16) | copy-start | bytes 12292
  13.9 28.5 %all-to-all-start = ((bf16[16,48,1024]{2,1,0:T(8,128)(2,1)}), bf16[16,48,1024]{2,1,0:T(8,128)(2,1)}, u32[]{:S(2)}, u32[]{:S(2)}) async-start(bf16[16,48,1024]{2,1,0:T(8,128)(2,1)} %bitcast.79), calls=%async_computation | async-start | bytes 3145728 | tf_op jit(solution)/shard_map/all_to_all | solution.py:46
  42.3 5.9 %copy-start.5 = (bf16[1,1024,2048]{2,1,0:T(8,128)(2,1)S(1)}, bf16[1,1024,2048]{2,1,0:T(8,128)(2,1)}, u32[]{:S(2)}) copy-start(bf16[1,1024,2048]{2,1,0:T(8,128)(2,1)} %param.17) | copy-start | bytes 12582916
  51.7 2.7 copy-start.2
  81.6 2.0 copy-start.3
  217.3 4.7 %copy-start.6 = (f32[1,1024]{1,0:T(1,128)S(1)}, f32[1,1024]{1,0:T(1,128)}, u32[]{:S(2)}) copy-start(f32[1,1024]{1,0:T(1,128)} %param.18) | copy-start | bytes 12292
  219.4 2.8 %copy-start.1 = (f32[768,1024]{1,0:T(8,128)S(1)}, f32[768,1024]{1,0:T(8,128)}, u32[]{:S(2)}) copy-start(f32[768,1024]{1,0:T(8,128)} %copy.17) | copy-start | bytes 9437188
  227.9 29.4 %all-to-all-start.1 = ((bf16[16,48,1024]{2,1,0:T(8,128)(2,1)}), bf16[16,48,1024]{2,1,0:T(8,128)(2,1)}, u32[]{:S(2)}, u32[]{:S(2)}) async-start(bf16[16,48,1024]{2,1,0:T(8,128)(2,1)} %bitcast.80), calls=%async_computation.1 | async-start | bytes 3145728 | tf_op jit(solution)/shard_map/all_to_all | solution.py:86
Sparse Core Ops, SparseCore 0:
  9.2 60.1 all-gather.2
where the time goes:
time: 271 us; the launch traced here: 269 us
  other arithmetic  76.3 us (28%)
  waiting for transfers between devices  57.2 us (21%)
  local copies, waits for them, and re-layouts  49.2 us (18%)
  matrix products  46.8 us (17%)
  starting transfers between devices  14.3 us (5%)
  between operations  13.5 us (5%)
  loops' own time  11.7 us (4%)
    add x8, other arithmetic, score_block(): return running + combined.reshape(running.shape)  39.8 us
    dot_general x8, matrix products, score_block(): jnp.einsum('hsk,khd->shd', attn_weights, value_heads, preferred_element_t...  37.8 us
    all_to_all x1, waiting for transfers between devices, on_device(): lax.all_to_all(hidden.reshape(owner_count, slot_cap, feat_width), 'users'...  22.9 us
    reduce_sum x16, other arithmetic, walk_block(): is_live = jnp.sum(jnp.where(block_range == block_id, block_mask, 0))  21.5 us
    all_to_all x1, waiting for transfers between devices, on_device(): lax.all_to_all(outgoing.reshape(owner_count, slot_cap, feat_width), 'user...  20.7 us
    unnamed x15, local copies, waits for them, and re-layouts  15.2 us
    all_gather x1, waiting for transfers between devices, on_device(): shard_rows = lax.all_gather(local_kv, 'ctx', axis=0, tiled=True)  13 us
    another operation x1, loops' own time, on_device(): result, unused = lax.scan(walk_block, zero_sum, (key_blocks, block_ids))  11.4 us
  transfers between devices with their start and end apart: 3, of which 3 were waited for; matrix products, arithmetic and copies ran while one was open for 7% of the time, Pallas kernels for 0%

commit v1 on v0

v1 whole, which is shorter than its diff:
```python
import jax
import jax.numpy as jnp
from jax import lax
from jax.experimental import pallas as pl
from jax.experimental.pallas import tpu as pltpu
from jax.sharding import PartitionSpec as P

H = 8
HD = 128
D = H * HD
BLK = 128
LIVE = 8
ROWS = 384
USERS = 16
CTX = 16
RING = 8
CAP = 48
SLOTS = USERS * CAP
HALF = LIVE * BLK // 2
GROUPS = ((0,), (1, 2), (3, 4), (5, 6), (7,))
MESH = pl.DeviceIdType.MESH
F32 = jnp.float32
BF16 = jnp.bfloat16


def silu(v):
    half = 0.5 * v
    return half + half * jnp.tanh(half)


def partner_user(me_u, d):
    step = lax.rem(d * 7, USERS)
    nx = lax.rem(lax.div(me_u, 4) + lax.div(step, 4), 4)
    ny = lax.rem(lax.rem(me_u, 4) + lax.rem(step, 4), 4)
    return nx * 4 + ny


def slot_rows(user):
    return pl.ds(pl.multiple_of(user * CAP, CAP), CAP)


def kernel(
    x_hbm, usr_ref, kv_hbm, mask_ref, gin_ref, wuq_hbm, gattn_ref, wout_hbm, out_ref,
    xv, wq, wg, wo, landed, kv, normed, qh, qs, qr, asend, arecv, acc, att, gate, disp, comb,
    lsem, a_send, a_recv, q_send, q_recv, t_send, t_recv,
    r_send, l_send, s_send, r_recv, l_recv, so_recv, sr_recv, sl_recv,
):
    me_u = lax.axis_index("users")
    me_c = lax.axis_index("ctx")
    z = lax.div(me_c, 2)
    core = lax.rem(me_c, 2)

    def column_of(ctx):
        return pl.multiple_of(lax.rem(ctx, 2) * D + lax.div(ctx, 2) * HD, HD)

    load_x = pltpu.make_async_copy(x_hbm, xv, lsem.at[0])
    load_wq = pltpu.make_async_copy(wuq_hbm.at[0, :, pl.ds(D, D)], wq, lsem.at[1])
    load_wg = pltpu.make_async_copy(wuq_hbm.at[0, :, pl.ds(0, D)], wg, lsem.at[2])
    load_wo = pltpu.make_async_copy(wout_hbm.at[0], wo, lsem.at[3])
    load_own = pltpu.make_async_copy(
        kv_hbm.at[0, 0, :, pl.ds(column_of(me_c), HD)], landed.at[me_c], lsem.at[4]
    )
    for load in (load_x, load_wq, load_own, load_wg, load_wo):
        load.start()

    barrier = pltpu.get_barrier_semaphore()

    def greet(d, carry):
        pl.semaphore_signal(
            barrier, inc=1, device_id={"ctx": lax.rem(me_c + d, CTX)}, device_id_type=MESH
        )
        pl.semaphore_signal(
            barrier, inc=1, device_id={"users": lax.rem(me_u + d, USERS)}, device_id_type=MESH
        )
        return carry

    lax.fori_loop(1, 16, greet, 0)
    pl.semaphore_wait(barrier, 30)

    def send_block(d, carry):
        dst = lax.rem(me_c + lax.rem(d * 7, CTX), CTX)
        pltpu.make_async_remote_copy(
            src_ref=kv_hbm.at[0, 0, :, pl.ds(column_of(dst), HD)],
            dst_ref=landed.at[me_c],
            send_sem=a_send,
            recv_sem=a_recv,
            device_id={"ctx": dst},
            device_id_type=MESH,
        ).start()
        return carry

    lax.fori_loop(1, CTX, send_block, 0)

    users = usr_ref[...]
    one_hot = (users == lax.broadcasted_iota(jnp.int32, (ROWS, 128), 1)).astype(F32)
    row_id = lax.broadcasted_iota(jnp.int32, (ROWS, ROWS), 0)
    col_id = lax.broadcasted_iota(jnp.int32, (ROWS, ROWS), 1)
    before = (col_id < row_id).astype(F32).astype(BF16)
    earlier = jnp.dot(before, one_hot.astype(BF16), preferred_element_type=F32)
    rank = jnp.sum(earlier * one_hot, axis=1, keepdims=True)
    slot = users.astype(F32) * CAP + rank
    slot_row = jnp.sum(jnp.where(row_id == col_id, slot, 0.0), axis=0, keepdims=True)
    comb[...] = (
        (lax.broadcasted_iota(jnp.int32, (ROWS, SLOTS), 1).astype(F32) == slot)
        .astype(F32).astype(BF16)
    )
    disp[...] = (
        (lax.broadcasted_iota(jnp.int32, (SLOTS, ROWS), 0).astype(F32) == slot_row)
        .astype(F32).astype(BF16)
    )

    load_x.wait()

    def norm_rows(t, carry):
        rows = pl.ds(pl.multiple_of(t * 64, 64), 64)
        value = xv[rows, :].astype(F32)
        shifted = value - jnp.mean(value, axis=1, keepdims=True)
        spread = jnp.mean(shifted * shifted, axis=1, keepdims=True)
        normed[rows, :] = (shifted * lax.rsqrt(spread + 1e-05) * gin_ref[...]).astype(BF16)
        return carry

    lax.fori_loop(0, ROWS // 64, norm_rows, 0)
    load_wq.wait()

    def project_query(n, carry):
        cols = pl.ds(pl.multiple_of(n * 256, 256), 256)
        value = silu(jnp.dot(normed[...], wq[:, cols], preferred_element_type=F32)).astype(BF16)
        qh[2 * n] = value[:, :HD]
        qh[2 * n + 1] = value[:, HD:]
        return carry

    lax.fori_loop(0, H // 2, project_query, 0)

    def head_at(order):
        offset = 0 if order == 0 else (-((order + 1) // 2) if order % 2 else order // 2)
        return lax.rem(z + (offset + RING), RING)

    def exchange(group, source, target, send_sem, recv_sem):
        first, count = group[0], len(group)

        def send(d, carry):
            dst = partner_user(me_u, d)
            pltpu.make_async_remote_copy(
                src_ref=source.at[pl.ds(first, count), slot_rows(dst), :],
                dst_ref=target.at[pl.ds(first, count), slot_rows(me_u), :],
                send_sem=send_sem,
                recv_sem=recv_sem,
                device_id={"users": dst},
                device_id_type=MESH,
            ).start()
            return carry

        lax.fori_loop(1, USERS, send, 0)
        for order in group:
            target[order, slot_rows(me_u), :] = source[order, slot_rows(me_u), :]

    def exchange_wait(group, buffer, sem):
        part = buffer.at[pl.ds(group[0], len(group)), pl.ds(0, SLOTS - CAP), :]
        pltpu.make_async_copy(part, part, sem).wait()

    for g, group in enumerate(GROUPS):
        heads = [qh[head_at(order)] for order in group]
        picked = heads[0] if len(group) == 1 else jnp.concatenate(heads, axis=1)
        routed = jnp.dot(disp[...], picked, preferred_element_type=F32).astype(BF16)
        for at, order in enumerate(group):
            qs[order] = routed[:, at * HD:(at + 1) * HD]
        exchange(group, qs, qr, q_send.at[g], q_recv.at[g])

    load_wg.wait()

    def project_gate(n, carry):
        cols = pl.ds(pl.multiple_of(n * 256, 256), 256)
        gate[:, cols] = silu(jnp.dot(normed[...], wg[:, cols], preferred_element_type=F32))
        return carry

    lax.fori_loop(0, H // 2, project_gate, 0)

    counts = []
    running = jnp.int32(0)
    for b in range(CTX):
        running = running + mask_ref[0, b]
        counts.append(running)
    load_own.wait()
    got = landed.at[pl.ds(0, CTX - 1)]
    pltpu.make_async_copy(got, got, a_recv).wait()

    def piece(lane, head, half):
        return lane * 2 * RING + head * 2 + half

    for r in range(LIVE):
        block = jnp.int32(0)
        for b in range(CTX):
            block = block + (counts[b] <= r).astype(jnp.int32)
        block = jnp.minimum(block, CTX - 1)
        kv[piece(core, z, r // 4), pl.ds((r % 4) * BLK, BLK), :] = landed[block]

    right = {"ctx": lax.rem(z + 1, RING) * 2 + core}
    left = {"ctx": lax.rem(z + RING - 1, RING) * 2 + core}
    sibling = {"ctx": z * 2 + 1 - core}

    def pass_on(at, to, send_sem, recv_sem):
        pltpu.make_async_remote_copy(
            src_ref=kv.at[at], dst_ref=kv.at[at], send_sem=send_sem, recv_sem=recv_sem,
            device_id=to, device_id_type=MESH,
        ).start()

    def arrived(at, sem):
        pltpu.make_async_copy(kv.at[at], kv.at[at], sem).wait()

    pass_on(piece(core, z, 0), right, r_send, r_recv.at[0])
    pass_on(piece(core, z, 1), left, l_send, l_recv.at[0])
    pass_on(piece(core, z, 0), sibling, s_send, so_recv.at[0])
    pass_on(piece(core, z, 1), sibling, s_send, so_recv.at[1])
    pass_on(piece(core, z, 1), right, r_send, r_recv.at[1])
    pass_on(piece(core, z, 0), left, l_send, l_recv.at[1])

    scale = 0.5 * HD ** (-0.5)
    row_tile = 384

    def attend(order, half, opening):
        head = head_at(order)
        key_at, value_at = piece(0, head, half), piece(1, head, half)

        def rows_of(t, carry):
            rows = pl.ds(pl.multiple_of(t * row_tile, row_tile), row_tile)
            scores = lax.dot_general(
                qr[order, rows, :], kv[key_at], (((1,), (1,)), ((), ())),
                preferred_element_type=F32,
            ) * scale
            weights = (scores + scores * jnp.tanh(scores)).astype(BF16)
            value = jnp.dot(weights, kv[value_at], preferred_element_type=F32)
            if opening:
                acc[order, rows, :] = value
            else:
                asend[order, rows, :] = (acc[order, rows, :] + value).astype(BF16)
            return carry

        lax.fori_loop(0, SLOTS // row_tile, rows_of, 0)

    def send_attended(g):
        exchange(GROUPS[g], asend, arecv, t_send.at[g], t_recv.at[g])

    exchange_wait(GROUPS[0], qr, q_recv.at[0])
    for half in range(2):
        arrived(piece(1 - core, z, half), so_recv.at[half])
        attend(0, half, half == 0)
    send_attended(0)

    def units_of(i):
        s, first = i // 2 + 1, i % 2
        if s == 4:
            return ((7, 0), (7, 1))
        return ((2 * s - 1, first), (2 * s, 1 - first))

    def finish(i):
        s = i // 2 + 1
        opening = i % 2 == 0
        if opening:
            exchange_wait(GROUPS[s], qr, q_recv.at[s])
        (lo, lo_half), (hi, hi_half) = units_of(i)
        arrived(piece(1 - core, head_at(lo), lo_half), sr_recv.at[i])
        attend(lo, lo_half, opening)
        arrived(piece(1 - core, head_at(hi), hi_half), sl_recv.at[i])
        attend(hi, hi_half, opening and s < 4)
        if not opening or s == 4:
            send_attended(s)

    for i in range(7):
        (lo, lo_half), (hi, hi_half) = units_of(i)
        from_left = piece(core, head_at(lo), lo_half)
        from_right = piece(core, head_at(hi), hi_half)
        onward = i + 2 if i < 5 else None
        arrived(from_left, r_recv.at[i])
        if onward is not None and (onward < 6 or i == 4):
            pass_on(from_left, right, r_send, r_recv.at[onward])
        pass_on(from_left, sibling, s_send, sr_recv.at[i])
        arrived(from_right, l_recv.at[i])
        if onward is not None and (onward < 6 or i == 4):
            pass_on(from_right, left, l_send, l_recv.at[onward])
        pass_on(from_right, sibling, s_send, sl_recv.at[i])
        if i > 0:
            finish(i - 1)
    finish(6)

    for g, group in enumerate(GROUPS):
        exchange_wait(group, arecv, t_recv.at[g])
        parts = [arecv[order] for order in group]
        packed = parts[0] if len(group) == 1 else jnp.concatenate(parts, axis=1)
        own = jnp.dot(comb[...], packed, preferred_element_type=F32)
        for at, order in enumerate(group):
            att[head_at(order)] = own[:, at * HD:(at + 1) * HD]

    def mix_rows(t, carry):
        rows = pl.ds(pl.multiple_of(t * 64, 64), 64)
        value = jnp.concatenate([att[h, rows, :] for h in range(H)], axis=1)
        shifted = value - jnp.mean(value, axis=1, keepdims=True)
        spread = jnp.mean(shifted * shifted, axis=1, keepdims=True)
        normed[rows, :] = (
            shifted * lax.rsqrt(spread + 1e-05) * gattn_ref[...] * gate[rows, :]
        ).astype(BF16)
        return carry

    lax.fori_loop(0, ROWS // 64, mix_rows, 0)
    load_wo.wait()

    def project_out(n, carry):
        cols = pl.ds(pl.multiple_of(n * 256, 256), 256)
        value = jnp.dot(normed[...], wo[:, cols], preferred_element_type=F32)
        out_ref[:, cols] = (xv[:, cols].astype(F32) + value).astype(BF16)
        return carry

    lax.fori_loop(0, D // 256, project_out, 0)

    sent = landed.at[pl.ds(0, CTX - 1)]
    pltpu.make_async_copy(sent, sent, a_send).wait()
    for g, group in enumerate(GROUPS):
        exchange_wait(group, qs, q_send.at[g])
        exchange_wait(group, asend, t_send.at[g])
    for sem, count in ((r_send, 7), (l_send, 7), (s_send, 16)):
        moved = kv.at[pl.ds(0, count)]
        pltpu.make_async_copy(moved, moved, sem).wait()


def on_device(cand_feat, cand_user, hist_kv, hist_mask, gain_in, w_uq, gain_attn, w_out):
    anywhere = pl.BlockSpec(memory_space=pl.ANY)
    vmem = pl.BlockSpec(memory_space=pltpu.VMEM)
    dma = pltpu.SemaphoreType.DMA
    return pl.pallas_call(
        kernel,
        out_shape=jax.ShapeDtypeStruct((ROWS, D), BF16),
        in_specs=[
            anywhere, vmem, anywhere, pl.BlockSpec(memory_space=pltpu.SMEM),
            vmem, anywhere, vmem, anywhere,
        ],
        out_specs=vmem,
        scratch_shapes=[
            pltpu.VMEM((ROWS, D), BF16),
            pltpu.VMEM((D, D), BF16),
            pltpu.VMEM((D, D), BF16),
            pltpu.VMEM((D, D), BF16),
            pltpu.VMEM((CTX, BLK, HD), BF16),
            pltpu.VMEM((2 * 2 * RING, HALF, HD), BF16),
            pltpu.VMEM((ROWS, D), BF16),
            pltpu.VMEM((H, ROWS, HD), BF16),
            pltpu.VMEM((H, SLOTS, HD), BF16),
            pltpu.VMEM((H, SLOTS, HD), BF16),
            pltpu.VMEM((H, SLOTS, HD), BF16),
            pltpu.VMEM((H, SLOTS, HD), BF16),
            pltpu.VMEM((H, SLOTS, HD), F32),
            pltpu.VMEM((H, ROWS, HD), F32),
            pltpu.VMEM((ROWS, D), F32),
            pltpu.VMEM((SLOTS, ROWS), BF16),
            pltpu.VMEM((ROWS, SLOTS), BF16),
            dma((5,)), dma(()), dma(()), dma((5,)), dma((5,)), dma((5,)), dma((5,)),
            dma(()), dma(()), dma(()), dma((7,)), dma((7,)), dma((2,)), dma((7,)), dma((7,)),
        ],
        compiler_params=pltpu.CompilerParams(
            collective_id=0, has_side_effects=True, vmem_limit_bytes=56 * 1024 * 1024
        ),
    )(cand_feat, cand_user, hist_kv, hist_mask, gain_in, w_uq, gain_attn, w_out)


def solution(mesh):
    in_specs = (
        P(("users", "ctx"), None),
        P(("users", "ctx"), None),
        P(None, "users", "ctx", None),
        P("users", None),
        P(),
        P(),
        P(),
        P(),
    )
    out_specs = P(("users", "ctx"), None)
    return jax.shard_map(
        on_device, mesh=mesh, in_specs=in_specs, out_specs=out_specs, check_vma=False
    )
```

time: 271 us -> 67.4 us (0.25)
  other arithmetic: 76.3 us -> 0 us
  Pallas kernels: 0 us -> 63.6 us
  waiting for transfers between devices: 57.2 us -> 0 us
  matrix products: 46.8 us -> 0 us
  local copies, waits for them, and re-layouts: 49.2 us -> 3.56 us
  starting transfers between devices: 14.3 us -> 0 us
  between operations: 13.5 us -> 0.01 us
  loops' own time: 11.7 us -> 0 us
    pallas_call x0 -> x1, Pallas kernels: none -> 63.6 us  [on_device(): pl.pallas_call(kernel, out_shape=jax.ShapeDtypeStruct((ROWS, D), BF16), i...]
    dot_general x10 -> x0, matrix products: 46.8 us -> none  [the longest x8 37.8 us: score_block(): jnp.einsum('hsk,khd->shd', attn_weights, value_heads, preferred_element_t...]
    all_to_all x2 -> x0, waiting for transfers between devices: 43.5 us -> none  [the longest x1 22.9 us: on_device(): lax.all_to_all(hidden.reshape(owner_count, slot_cap, feat_width), 'users'...]
    add x8 -> x0, other arithmetic: 39.8 us -> none  [score_block(): return running + combined.reshape(running.shape)]
    reduce_sum x21 -> x0, other arithmetic: 30.1 us -> none  [the longest x16 21.5 us: walk_block(): is_live = jnp.sum(jnp.where(block_range == block_id, block_mask, 0))]
    all_to_all x2 -> x0, starting transfers between devices: 14.3 us -> none  [the longest x1 7.77 us: on_device(): lax.all_to_all(outgoing.reshape(owner_count, slot_cap, feat_width), 'user...]
    all_gather x1 -> x0, waiting for transfers between devices: 13 us -> none  [on_device(): shard_rows = lax.all_gather(local_kv, 'ctx', axis=0, tiled=True)]
    another operation x17 -> x0, loops' own time: 11.7 us -> none  [the longest x1 11.4 us: on_device(): result, unused = lax.scan(walk_block, zero_sum, (key_blocks, block_ids))]
  transfers between devices with their start and end apart: 3 -> 0, of which waited for: 3 -> 0; matrix products, arithmetic and copies ran while one was open for 7% -> 0% of each run, Pallas kernels for 0% -> 0%
where the time goes in v1:
time: 67.4 us; the launch traced here: 67.2 us
  Pallas kernels  63.6 us (94%)
  local copies, waits for them, and re-layouts  3.56 us (5%)
    pallas_call x1, Pallas kernels, on_device(): pl.pallas_call(kernel, out_shape=jax.ShapeDtypeStruct((ROWS, D), BF16), i...  63.6 us
    unnamed x2, local copies, waits for them, and re-layouts  3.56 us

profile of v1, /device:TPU:1, one launch (start us, length us, event | category | flops | bytes accessed | tf_op | source)
XLA Modules:
  0.0 67.2 jit_solution(1027832101159802802)
XLA Ops:
  0.0 1.5 %copy.9.usr_ref = s32[384,1]{1,0:T(8,128)} copy(s32[384,1]{0,1:T(1,128)} %param.9) | data formatting | bytes 3072 | tf_op args[1]
  1.5 63.6 %shard_map.82 = bf16[384,1024]{1,0:T(8,128)(2,1)} custom-call(bf16[384,1024]{1,0:T(8,128)(2,1)} %x_hbm.1, s32[384,1]{1,0:T(8,128)} %copy.9.usr_ref, bf16[1,1,128,2048]{3,2,1,0:T(8,128)(2,1)} %kv_hbm.1, s32[1,16]{1,0:T(1,128)} %mask_ref.1, f32[1,1024]{1,0:T(1,128)} %gin_ref.1, bf16[1,1024,2048]{2,1,0:T(8,128)(2,1)} %wuq_hbm.1, f32[1,1024]{1,0:T(1,128)} %gattn_ref.1, ...), custom_call_target="tpu_custom_call" | custom-call | tf_op jit(solution)/shard_map/pallas_call | solution.py:328
  65.1 2.1 %copy.11 = bf16[384,1024]{1,0:T(8,128)(2,1)} copy(bf16[384,1024]{1,0:T(8,128)(2,1)} %shard_map.82) | data formatting | bytes 1572864

commit v2 on v1

--- a/solution.py
+++ b/solution.py
@@ -40,9 +40,9 @@
 
 
 def kernel(
-    x_hbm, usr_ref, kv_hbm, mask_ref, gin_ref, wuq_hbm, gattn_ref, wout_hbm, out_ref,
-    xv, wq, wg, wo, landed, kv, normed, qh, qs, qr, asend, arecv, acc, att, gate, disp, comb,
-    lsem, a_send, a_recv, q_send, q_recv, t_send, t_recv,
+    x_hbm, usr_ref, kv_hbm, mask_ref, gin_ref, wuq_hbm, gattn_ref, mixed_ref,
+    xv, wq, wg, landed_a, landed_b, kv, normed, qs, qr, asend, arecv, acc, att, gate, disp, comb,
+    lsem, wsem, a_send, a_recv, q_send, q_recv, t_send, t_recv,
     r_send, l_send, s_send, r_recv, l_recv, so_recv, sr_recv, sl_recv,
 ):
     me_u = lax.axis_index("users")
@@ -53,15 +53,36 @@
     def column_of(ctx):
         return pl.multiple_of(lax.rem(ctx, 2) * D + lax.div(ctx, 2) * HD, HD)
 
+    def head_at(order):
+        offset = 0 if order == 0 else (-((order + 1) // 2) if order % 2 else order // 2)
+        return lax.rem(z + (offset + RING), RING)
+
+    def load_query_weight(order):
+        column = pl.multiple_of(D + head_at(order) * HD, HD)
+        return pltpu.make_async_copy(
+            wuq_hbm.at[0, :, pl.ds(column, HD)], wq.at[order], wsem.at[order]
+        )
+
     load_x = pltpu.make_async_copy(x_hbm, xv, lsem.at[0])
-    load_wq = pltpu.make_async_copy(wuq_hbm.at[0, :, pl.ds(D, D)], wq, lsem.at[1])
-    load_wg = pltpu.make_async_copy(wuq_hbm.at[0, :, pl.ds(0, D)], wg, lsem.at[2])
-    load_wo = pltpu.make_async_copy(wout_hbm.at[0], wo, lsem.at[3])
-    load_own = pltpu.make_async_copy(
-        kv_hbm.at[0, 0, :, pl.ds(column_of(me_c), HD)], landed.at[me_c], lsem.at[4]
-    )
-    for load in (load_x, load_wq, load_own, load_wg, load_wo):
-        load.start()
+    load_wg = pltpu.make_async_copy(wuq_hbm.at[0, :, pl.ds(0, D)], wg, lsem.at[1])
+    landed = (landed_a, landed_b)
+
+    def half_rows(half):
+        return pl.ds(half * (BLK // 2), BLK // 2)
+
+    def load_own(half):
+        return pltpu.make_async_copy(
+            kv_hbm.at[0, 0, half_rows(half), pl.ds(column_of(me_c), HD)],
+            landed[half].at[me_c],
+            lsem.at[2 + half],
+        )
+
+    load_x.start()
+    for order in range(H):
+        load_query_weight(order).start()
+    for half in range(2):
+        load_own(half).start()
+    load_wg.start()
 
     barrier = pltpu.get_barrier_semaphore()
 
@@ -77,28 +98,38 @@
     lax.fori_loop(1, 16, greet, 0)
     pl.semaphore_wait(barrier, 30)
 
-    def send_block(d, carry):
-        dst = lax.rem(me_c + lax.rem(d * 7, CTX), CTX)
-        pltpu.make_async_remote_copy(
-            src_ref=kv_hbm.at[0, 0, :, pl.ds(column_of(dst), HD)],
-            dst_ref=landed.at[me_c],
-            send_sem=a_send,
-            recv_sem=a_recv,
-            device_id={"ctx": dst},
-            device_id_type=MESH,
-        ).start()
-        return carry
-
-    lax.fori_loop(1, CTX, send_block, 0)
-
-    users = usr_ref[...]
-    one_hot = (users == lax.broadcasted_iota(jnp.int32, (ROWS, 128), 1)).astype(F32)
+    def send_blocks(half):
+        def send(d, carry):
+            dst = lax.rem(me_c + lax.rem(d * 7, CTX), CTX)
+            pltpu.make_async_remote_copy(
+                src_ref=kv_hbm.at[0, 0, half_rows(half), pl.ds(column_of(dst), HD)],
+                dst_ref=landed[half].at[me_c],
+                send_sem=a_send.at[half],
+                recv_sem=a_recv.at[half],
+                device_id={"ctx": dst},
+                device_id_type=MESH,
+            ).start()
+            return carry
+
+        lax.fori_loop(1, CTX, send, 0)
+
+    def blocks_wait(half, sem):
+        got = landed[half].at[pl.ds(0, CTX - 1)]
+        pltpu.make_async_copy(got, got, sem.at[half]).wait()
+
+    send_blocks(0)
+    send_blocks(1)
+
     row_id = lax.broadcasted_iota(jnp.int32, (ROWS, ROWS), 0)
     col_id = lax.broadcasted_iota(jnp.int32, (ROWS, ROWS), 1)
+    users = jnp.sum(
+        jnp.where(row_id == col_id, usr_ref[...].astype(F32), 0.0), axis=1, keepdims=True
+    )
+    one_hot = (users == lax.broadcasted_iota(jnp.int32, (ROWS, 128), 1).astype(F32)).astype(F32)
     before = (col_id < row_id).astype(F32).astype(BF16)
     earlier = jnp.dot(before, one_hot.astype(BF16), preferred_element_type=F32)
     rank = jnp.sum(earlier * one_hot, axis=1, keepdims=True)
-    slot = users.astype(F32) * CAP + rank
+    slot = users * CAP + rank
     slot_row = jnp.sum(jnp.where(row_id == col_id, slot, 0.0), axis=0, keepdims=True)
     comb[...] = (
         (lax.broadcasted_iota(jnp.int32, (ROWS, SLOTS), 1).astype(F32) == slot)
@@ -120,21 +151,6 @@
         return carry
 
     lax.fori_loop(0, ROWS // 64, norm_rows, 0)
-    load_wq.wait()
-
-    def project_query(n, carry):
-        cols = pl.ds(pl.multiple_of(n * 256, 256), 256)
-        value = silu(jnp.dot(normed[...], wq[:, cols], preferred_element_type=F32)).astype(BF16)
-        qh[2 * n] = value[:, :HD]
-        qh[2 * n + 1] = value[:, HD:]
-        return carry
-
-    lax.fori_loop(0, H // 2, project_query, 0)
-
-    def head_at(order):
-        offset = 0 if order == 0 else (-((order + 1) // 2) if order % 2 else order // 2)
-        return lax.rem(z + (offset + RING), RING)
-
     def exchange(group, source, target, send_sem, recv_sem):
         first, count = group[0], len(group)
 
@@ -159,9 +175,12 @@
         pltpu.make_async_copy(part, part, sem).wait()
 
     for g, group in enumerate(GROUPS):
-        heads = [qh[head_at(order)] for order in group]
-        picked = heads[0] if len(group) == 1 else jnp.concatenate(heads, axis=1)
-        routed = jnp.dot(disp[...], picked, preferred_element_type=F32).astype(BF16)
+        for order in group:
+            load_query_weight(order).wait()
+        weights = [wq[order] for order in group]
+        weight = weights[0] if len(group) == 1 else jnp.concatenate(weights, axis=1)
+        query = silu(jnp.dot(normed[...], weight, preferred_element_type=F32)).astype(BF16)
+        routed = jnp.dot(disp[...], query, preferred_element_type=F32).astype(BF16)
         for at, order in enumerate(group):
             qs[order] = routed[:, at * HD:(at + 1) * HD]
         exchange(group, qs, qr, q_send.at[g], q_recv.at[g])
@@ -180,19 +199,15 @@
     for b in range(CTX):
         running = running + mask_ref[0, b]
         counts.append(running)
-    load_own.wait()
-    got = landed.at[pl.ds(0, CTX - 1)]
-    pltpu.make_async_copy(got, got, a_recv).wait()
-
-    def piece(lane, head, half):
-        return lane * 2 * RING + head * 2 + half
-
+    live = []
     for r in range(LIVE):
         block = jnp.int32(0)
         for b in range(CTX):
             block = block + (counts[b] <= r).astype(jnp.int32)
-        block = jnp.minimum(block, CTX - 1)
-        kv[piece(core, z, r // 4), pl.ds((r % 4) * BLK, BLK), :] = landed[block]
+        live.append(jnp.minimum(block, CTX - 1))
+
+    def piece(lane, head, half):
+        return lane * 2 * RING + head * 2 + half
 
     right = {"ctx": lax.rem(z + 1, RING) * 2 + core}
     left = {"ctx": lax.rem(z + RING - 1, RING) * 2 + core}
@@ -207,12 +222,15 @@
     def arrived(at, sem):
         pltpu.make_async_copy(kv.at[at], kv.at[at], sem).wait()
 
-    pass_on(piece(core, z, 0), right, r_send, r_recv.at[0])
-    pass_on(piece(core, z, 1), left, l_send, l_recv.at[0])
-    pass_on(piece(core, z, 0), sibling, s_send, so_recv.at[0])
-    pass_on(piece(core, z, 1), sibling, s_send, so_recv.at[1])
-    pass_on(piece(core, z, 1), right, r_send, r_recv.at[1])
-    pass_on(piece(core, z, 0), left, l_send, l_recv.at[1])
+    for half in range(2):
+        load_own(half).wait()
+        blocks_wait(half, a_recv)
+        own = piece(core, z, half)
+        for r in range(LIVE):
+            kv[own, pl.ds(r * (BLK // 2), BLK // 2), :] = landed[half][live[r]]
+        pass_on(own, right, r_send, r_recv.at[half])
+        pass_on(own, left, l_send, l_recv.at[half])
+        pass_on(own, sibling, s_send, so_recv.at[half])
 
     scale = 0.5 * HD ** (-0.5)
     row_tile = 384
@@ -250,7 +268,7 @@
         s, first = i // 2 + 1, i % 2
         if s == 4:
             return ((7, 0), (7, 1))
-        return ((2 * s - 1, first), (2 * s, 1 - first))
+        return ((2 * s - 1, first), (2 * s, first))
 
     def finish(i):
         s = i // 2 + 1
@@ -269,14 +287,13 @@
         (lo, lo_half), (hi, hi_half) = units_of(i)
         from_left = piece(core, head_at(lo), lo_half)
         from_right = piece(core, head_at(hi), hi_half)
-        onward = i + 2 if i < 5 else None
         arrived(from_left, r_recv.at[i])
-        if onward is not None and (onward < 6 or i == 4):
-            pass_on(from_left, right, r_send, r_recv.at[onward])
+        if i < 5:
+            pass_on(from_left, right, r_send, r_recv.at[i + 2])
         pass_on(from_left, sibling, s_send, sr_recv.at[i])
         arrived(from_right, l_recv.at[i])
-        if onward is not None and (onward < 6 or i == 4):
-            pass_on(from_right, left, l_send, l_recv.at[onward])
+        if i < 4 or i == 5:
+            pass_on(from_right, left, l_send, l_recv.at[min(i + 2, 6)])
         pass_on(from_right, sibling, s_send, sl_recv.at[i])
         if i > 0:
             finish(i - 1)
@@ -295,24 +312,14 @@
         value = jnp.concatenate([att[h, rows, :] for h in range(H)], axis=1)
         shifted = value - jnp.mean(value, axis=1, keepdims=True)
         spread = jnp.mean(shifted * shifted, axis=1, keepdims=True)
-        normed[rows, :] = (
+        mixed_ref[rows, :] = (
             shifted * lax.rsqrt(spread + 1e-05) * gattn_ref[...] * gate[rows, :]
         ).astype(BF16)
         return carry
 
     lax.fori_loop(0, ROWS // 64, mix_rows, 0)
-    load_wo.wait()
-
-    def project_out(n, carry):
-        cols = pl.ds(pl.multiple_of(n * 256, 256), 256)
-        value = jnp.dot(normed[...], wo[:, cols], preferred_element_type=F32)
-        out_ref[:, cols] = (xv[:, cols].astype(F32) + value).astype(BF16)
-        return carry
-
-    lax.fori_loop(0, D // 256, project_out, 0)
-
-    sent = landed.at[pl.ds(0, CTX - 1)]
-    pltpu.make_async_copy(sent, sent, a_send).wait()
+    for half in range(2):
+        blocks_wait(half, a_send)
     for g, group in enumerate(GROUPS):
         exchange_wait(group, qs, q_send.at[g])
         exchange_wait(group, asend, t_send.at[g])
@@ -325,23 +332,22 @@
     anywhere = pl.BlockSpec(memory_space=pl.ANY)
     vmem = pl.BlockSpec(memory_space=pltpu.VMEM)
     dma = pltpu.SemaphoreType.DMA
-    return pl.pallas_call(
+    mixed = pl.pallas_call(
         kernel,
         out_shape=jax.ShapeDtypeStruct((ROWS, D), BF16),
         in_specs=[
             anywhere, vmem, anywhere, pl.BlockSpec(memory_space=pltpu.SMEM),
-            vmem, anywhere, vmem, anywhere,
+            vmem, anywhere, vmem,
         ],
         out_specs=vmem,
         scratch_shapes=[
             pltpu.VMEM((ROWS, D), BF16),
+            pltpu.VMEM((H, D, HD), BF16),
             pltpu.VMEM((D, D), BF16),
-            pltpu.VMEM((D, D), BF16),
-            pltpu.VMEM((D, D), BF16),
-            pltpu.VMEM((CTX, BLK, HD), BF16),
+            pltpu.VMEM((CTX, BLK // 2, HD), BF16),
+            pltpu.VMEM((CTX, BLK // 2, HD), BF16),
             pltpu.VMEM((2 * 2 * RING, HALF, HD), BF16),
             pltpu.VMEM((ROWS, D), BF16),
-            pltpu.VMEM((H, ROWS, HD), BF16),
             pltpu.VMEM((H, SLOTS, HD), BF16),
             pltpu.VMEM((H, SLOTS, HD), BF16),
             pltpu.VMEM((H, SLOTS, HD), BF16),
@@ -351,13 +357,15 @@
             pltpu.VMEM((ROWS, D), F32),
             pltpu.VMEM((SLOTS, ROWS), BF16),
             pltpu.VMEM((ROWS, SLOTS), BF16),
-            dma((5,)), dma(()), dma(()), dma((5,)), dma((5,)), dma((5,)), dma((5,)),
+            dma((4,)), dma((H,)), dma((2,)), dma((2,)), dma((5,)), dma((5,)), dma((5,)), dma((5,)),
             dma(()), dma(()), dma(()), dma((7,)), dma((7,)), dma((2,)), dma((7,)), dma((7,)),
         ],
         compiler_params=pltpu.CompilerParams(
             collective_id=0, has_side_effects=True, vmem_limit_bytes=56 * 1024 * 1024
         ),
-    )(cand_feat, cand_user, hist_kv, hist_mask, gain_in, w_uq, gain_attn, w_out)
+    )(cand_feat, cand_user.reshape(1, ROWS), hist_kv, hist_mask, gain_in, w_uq, gain_attn)
+    scored = jnp.dot(mixed, w_out[0], preferred_element_type=F32)
+    return (cand_feat.astype(F32) + scored).astype(BF16)
 
 
 def solution(mesh):

time: 67.4 us -> 62.7 us (0.930)
  Pallas kernels: 63.6 us -> 59.3 us
  local copies, waits for them, and re-layouts: 3.56 us -> 0.01 us
  matrix products: 0 us -> 3 us
    pallas_call x1, Pallas kernels: 63.6 us -> 59.3 us  [on_device(): pl.pallas_call(kernel, out_shape=jax.ShapeDtypeStruct((ROWS, D), BF16), i...]
    unnamed x2 -> x4, local copies, waits for them, and re-layouts: 3.56 us -> 0.01 us
    dot_general x0 -> x1, matrix products: none -> 3 us  [on_device(): scored = jnp.dot(mixed, w_out[0], preferred_element_type=F32)]
where the time goes in v2:
time: 62.7 us; the launch traced here: 62.3 us
  Pallas kernels  59.3 us (95%)
  matrix products  3 us (5%)
    pallas_call x1, Pallas kernels, on_device(): pl.pallas_call(kernel, out_shape=jax.ShapeDtypeStruct((ROWS, D), BF16), i...  59.3 us
    dot_general x1, matrix products, on_device(): scored = jnp.dot(mixed, w_out[0], preferred_element_type=F32)  3 us

profile of v2, /device:TPU:1, one launch (start us, length us, event | category | flops | bytes accessed | tf_op | source)
XLA Modules:
  0.0 62.3 jit_solution(5380745130754695950)
XLA Ops:
  0.0 0.0 copy-start
  0.0 0.0 copy-start.1
  0.0 59.3 %shard_map.82 = bf16[384,1024]{1,0:T(8,128)(2,1)} custom-call(bf16[384,1024]{1,0:T(8,128)(2,1)} %x_hbm.1, s32[1,384]{1,0:T(1,128)} %bitcast.7, bf16[1,1,128,2048]{3,2,1,0:T(8,128)(2,1)} %kv_hbm.1, s32[1,16]{1,0:T(1,128)} %mask_ref.1, f32[1,1024]{1,0:T(1,128)} %gin_ref.1, bf16[1,1024,2048]{2,1,0:T(8,128)(2,1)} %wuq_hbm.1, f32[1,1024]{1,0:T(1,128)} %gattn_ref.1), custom_call_target="tpu_custom_call" | custom-call | tf_op jit(solution)/shard_map/pallas_call | solution.py:335
  59.3 0.0 copy-done
  59.3 0.0 copy-done.1
  59.3 3.0 %add_convert_fusion = bf16[384,1024]{1,0:T(8,128)(2,1)} fusion(bf16[384,1024]{1,0:T(8,128)(2,1)S(1)} %copy-done.1, bf16[384,1024]{1,0:T(8,128)(2,1)} %shard_map.82, bf16[1,1024,1024]{2,1,0:T(8,128)(2,1)S(1)} %copy-done), kind=kOutput, calls=%fused_computation.2 | convolution fusion | flops 806486016 | bytes 4456448 | tf_op jit(solution)/shard_map/dot_general | solution.py:367
Async XLA Ops:
  0.0 59.3 %copy-start = (bf16[1,1024,1024]{2,1,0:T(8,128)(2,1)S(1)}, bf16[1,1024,1024]{2,1,0:T(8,128)(2,1)}, u32[]{:S(2)}) copy-start(bf16[1,1024,1024]{2,1,0:T(8,128)(2,1)} %param.15) | copy-start | bytes 6291460
  0.0 59.3 %copy-start.1 = (bf16[384,1024]{1,0:T(8,128)(2,1)S(1)}, bf16[384,1024]{1,0:T(8,128)(2,1)}, u32[]{:S(2)}) copy-start(bf16[384,1024]{1,0:T(8,128)(2,1)} %x_hbm.1) | copy-start | bytes 2359300

commit v3 on v2

--- a/solution.py
+++ b/solution.py
@@ -118,7 +118,6 @@
         pltpu.make_async_copy(got, got, sem.at[half]).wait()
 
     send_blocks(0)
-    send_blocks(1)
 
     row_id = lax.broadcasted_iota(jnp.int32, (ROWS, ROWS), 0)
     col_id = lax.broadcasted_iota(jnp.int32, (ROWS, ROWS), 1)
@@ -174,7 +173,8 @@
         part = buffer.at[pl.ds(group[0], len(group)), pl.ds(0, SLOTS - CAP), :]
         pltpu.make_async_copy(part, part, sem).wait()
 
-    for g, group in enumerate(GROUPS):
+    def route_queries(g):
+        group = GROUPS[g]
         for order in group:
             load_query_weight(order).wait()
         weights = [wq[order] for order in group]
@@ -183,8 +183,17 @@
         routed = jnp.dot(disp[...], query, preferred_element_type=F32).astype(BF16)
         for at, order in enumerate(group):
             qs[order] = routed[:, at * HD:(at + 1) * HD]
-        exchange(group, qs, qr, q_send.at[g], q_recv.at[g])
-
+
+    def send_queries(g):
+        exchange(GROUPS[g], qs, qr, q_send.at[g], q_recv.at[g])
+
+    route_queries(0)
+    send_queries(0)
+    route_queries(1)
+    send_queries(1)
+    blocks_wait(0, a_send)
+    send_blocks(1)
+    route_queries(2)
     load_wg.wait()
 
     def project_gate(n, carry):
@@ -231,38 +240,37 @@
         pass_on(own, right, r_send, r_recv.at[half])
         pass_on(own, left, l_send, l_recv.at[half])
         pass_on(own, sibling, s_send, so_recv.at[half])
+        if half == 0:
+            send_queries(2)
+            route_queries(3)
+            route_queries(4)
+    send_queries(3)
+    send_queries(4)
 
     scale = 0.5 * HD ** (-0.5)
-    row_tile = 384
 
     def attend(order, half, opening):
         head = head_at(order)
-        key_at, value_at = piece(0, head, half), piece(1, head, half)
-
-        def rows_of(t, carry):
-            rows = pl.ds(pl.multiple_of(t * row_tile, row_tile), row_tile)
-            scores = lax.dot_general(
-                qr[order, rows, :], kv[key_at], (((1,), (1,)), ((), ())),
-                preferred_element_type=F32,
-            ) * scale
-            weights = (scores + scores * jnp.tanh(scores)).astype(BF16)
-            value = jnp.dot(weights, kv[value_at], preferred_element_type=F32)
-            if opening:
-                acc[order, rows, :] = value
-            else:
-                asend[order, rows, :] = (acc[order, rows, :] + value).astype(BF16)
-            return carry
-
-        lax.fori_loop(0, SLOTS // row_tile, rows_of, 0)
+        scores = lax.dot_general(
+            qr[order], kv[piece(0, head, half)], (((1,), (1,)), ((), ())),
+            preferred_element_type=F32,
+        ) * scale
+        weights = (scores + scores * jnp.tanh(scores)).astype(BF16)
+        value = jnp.dot(weights, kv[piece(1, head, half)], preferred_element_type=F32)
+        if opening:
+            acc[order] = value
+        else:
+            asend[order] = (acc[order] + value).astype(BF16)
 
     def send_attended(g):
         exchange(GROUPS[g], asend, arecv, t_send.at[g], t_recv.at[g])
 
-    exchange_wait(GROUPS[0], qr, q_recv.at[0])
-    for half in range(2):
-        arrived(piece(1 - core, z, half), so_recv.at[half])
-        attend(0, half, half == 0)
-    send_attended(0)
+    def finish_first():
+        exchange_wait(GROUPS[0], qr, q_recv.at[0])
+        for half in range(2):
+            arrived(piece(1 - core, z, half), so_recv.at[half])
+            attend(0, half, half == 0)
+        send_attended(0)
 
     def units_of(i):
         s, first = i // 2 + 1, i % 2
@@ -295,8 +303,12 @@
         if i < 4 or i == 5:
             pass_on(from_right, left, l_send, l_recv.at[min(i + 2, 6)])
         pass_on(from_right, sibling, s_send, sl_recv.at[i])
-        if i > 0:
+        if i == 0:
+            finish_first()
+        elif i < 6:
             finish(i - 1)
+        if i == 5:
+            finish(5)
     finish(6)
 
     for g, group in enumerate(GROUPS):
@@ -318,8 +330,7 @@
         return carry
 
     lax.fori_loop(0, ROWS // 64, mix_rows, 0)
-    for half in range(2):
-        blocks_wait(half, a_send)
+    blocks_wait(1, a_send)
     for g, group in enumerate(GROUPS):
         exchange_wait(group, qs, q_send.at[g])
         exchange_wait(group, asend, t_send.at[g])

time: 62.7 us -> 62.9 us (level)
  no operation moved by 1% of the time
where the time goes in v3:
time: 62.9 us; the launch traced here: 62.8 us
  Pallas kernels  59.8 us (95%)
  matrix products  3 us (5%)
    pallas_call x1, Pallas kernels, on_device(): pl.pallas_call(kernel, out_shape=jax.ShapeDtypeStruct((ROWS, D), BF16), i...  59.8 us
    dot_general x1, matrix products, on_device(): scored = jnp.dot(mixed, w_out[0], preferred_element_type=F32)  3 us

profile of v3, /device:TPU:1, one launch (start us, length us, event | category | flops | bytes accessed | tf_op | source)
XLA Modules:
  0.0 62.8 jit_solution(3969474714847179336)
XLA Ops:
  0.0 0.0 copy-start
  0.0 0.0 copy-start.1
  0.0 59.8 %shard_map.82 = bf16[384,1024]{1,0:T(8,128)(2,1)} custom-call(bf16[384,1024]{1,0:T(8,128)(2,1)} %x_hbm.1, s32[1,384]{1,0:T(1,128)} %bitcast.7, bf16[1,1,128,2048]{3,2,1,0:T(8,128)(2,1)} %kv_hbm.1, s32[1,16]{1,0:T(1,128)} %mask_ref.1, f32[1,1024]{1,0:T(1,128)} %gin_ref.1, bf16[1,1024,2048]{2,1,0:T(8,128)(2,1)} %wuq_hbm.1, f32[1,1024]{1,0:T(1,128)} %gattn_ref.1), custom_call_target="tpu_custom_call" | custom-call | tf_op jit(solution)/shard_map/pallas_call | solution.py:346
  59.8 0.0 copy-done
  59.8 0.0 copy-done.1
  59.8 3.0 %add_convert_fusion = bf16[384,1024]{1,0:T(8,128)(2,1)} fusion(bf16[384,1024]{1,0:T(8,128)(2,1)S(1)} %copy-done.1, bf16[384,1024]{1,0:T(8,128)(2,1)} %shard_map.82, bf16[1,1024,1024]{2,1,0:T(8,128)(2,1)S(1)} %copy-done), kind=kOutput, calls=%fused_computation.2 | convolution fusion | flops 806486016 | bytes 4456448 | tf_op jit(solution)/shard_map/dot_general | solution.py:378
Async XLA Ops:
  0.0 59.8 %copy-start = (bf16[1,1024,1024]{2,1,0:T(8,128)(2,1)S(1)}, bf16[1,1024,1024]{2,1,0:T(8,128)(2,1)}, u32[]{:S(2)}) copy-start(bf16[1,1024,1024]{2,1,0:T(8,128)(2,1)} %param.15) | copy-start | bytes 6291460
  0.0 59.8 %copy-start.1 = (bf16[384,1024]{1,0:T(8,128)(2,1)S(1)}, bf16[384,1024]{1,0:T(8,128)(2,1)}, u32[]{:S(2)}) copy-start(bf16[384,1024]{1,0:T(8,128)(2,1)} %x_hbm.1) | copy-start | bytes 2359300

commit v4 on v3

--- a/solution.py
+++ b/solution.py
@@ -149,7 +149,7 @@
         normed[rows, :] = (shifted * lax.rsqrt(spread + 1e-05) * gin_ref[...]).astype(BF16)
         return carry
 
-    lax.fori_loop(0, ROWS // 64, norm_rows, 0)
+    lax.fori_loop(0, ROWS // 64, norm_rows, 0, unroll=True)
     def exchange(group, source, target, send_sem, recv_sem):
         first, count = group[0], len(group)
 
@@ -231,21 +231,30 @@
     def arrived(at, sem):
         pltpu.make_async_copy(kv.at[at], kv.at[at], sem).wait()
 
+    def quarter(at, sub):
+        return at, pl.ds(sub * (HALF // 2), HALF // 2)
+
+    def start_round(own, half, sub):
+        pass_on(quarter(own, sub), right, r_send, r_recv.at[half, sub])
+        pass_on(quarter(own, sub), left, l_send, l_recv.at[half, sub])
+
     for half in range(2):
         load_own(half).wait()
         blocks_wait(half, a_recv)
         own = piece(core, z, half)
         for r in range(LIVE):
             kv[own, pl.ds(r * (BLK // 2), BLK // 2), :] = landed[half][live[r]]
-        pass_on(own, right, r_send, r_recv.at[half])
-        pass_on(own, left, l_send, l_recv.at[half])
+        start_round(own, half, 0)
         pass_on(own, sibling, s_send, so_recv.at[half])
         if half == 0:
             send_queries(2)
             route_queries(3)
+            start_round(own, half, 1)
             route_queries(4)
-    send_queries(3)
-    send_queries(4)
+        else:
+            send_queries(3)
+            send_queries(4)
+            start_round(own, half, 1)
 
     scale = 0.5 * HD ** (-0.5)
 
@@ -295,13 +304,14 @@
         (lo, lo_half), (hi, hi_half) = units_of(i)
         from_left = piece(core, head_at(lo), lo_half)
         from_right = piece(core, head_at(hi), hi_half)
-        arrived(from_left, r_recv.at[i])
-        if i < 5:
-            pass_on(from_left, right, r_send, r_recv.at[i + 2])
+        for sub in range(2):
+            arrived(quarter(from_left, sub), r_recv.at[i, sub])
+            if i < 5:
+                pass_on(quarter(from_left, sub), right, r_send, r_recv.at[i + 2, sub])
+            arrived(quarter(from_right, sub), l_recv.at[i, sub])
+            if i < 4 or i == 5:
+                pass_on(quarter(from_right, sub), left, l_send, l_recv.at[min(i + 2, 6), sub])
         pass_on(from_left, sibling, s_send, sr_recv.at[i])
-        arrived(from_right, l_recv.at[i])
-        if i < 4 or i == 5:
-            pass_on(from_right, left, l_send, l_recv.at[min(i + 2, 6)])
         pass_on(from_right, sibling, s_send, sl_recv.at[i])
         if i == 0:
             finish_first()
@@ -329,7 +339,7 @@
         ).astype(BF16)
         return carry
 
-    lax.fori_loop(0, ROWS // 64, mix_rows, 0)
+    lax.fori_loop(0, ROWS // 64, mix_rows, 0, unroll=True)
     blocks_wait(1, a_send)
     for g, group in enumerate(GROUPS):
         exchange_wait(group, qs, q_send.at[g])
@@ -369,7 +379,7 @@
             pltpu.VMEM((SLOTS, ROWS), BF16),
             pltpu.VMEM((ROWS, SLOTS), BF16),
             dma((4,)), dma((H,)), dma((2,)), dma((2,)), dma((5,)), dma((5,)), dma((5,)), dma((5,)),
-            dma(()), dma(()), dma(()), dma((7,)), dma((7,)), dma((2,)), dma((7,)), dma((7,)),
+            dma(()), dma(()), dma(()), dma((7, 2)), dma((7, 2)), dma((2,)), dma((7,)), dma((7,)),
         ],
         compiler_params=pltpu.CompilerParams(
             collective_id=0, has_side_effects=True, vmem_limit_bytes=56 * 1024 * 1024

time: 62.9 us -> 62.4 us (level)
  no operation moved by 1% of the time
where the time goes in v4:
time: 62.4 us; the launch traced here: 62.2 us
  Pallas kernels  59.2 us (95%)
  matrix products  3 us (5%)
    pallas_call x1, Pallas kernels, on_device(): pl.pallas_call(kernel, out_shape=jax.ShapeDtypeStruct((ROWS, D), BF16), i...  59.2 us
    dot_general x1, matrix products, on_device(): scored = jnp.dot(mixed, w_out[0], preferred_element_type=F32)  3 us

profile of v4, /device:TPU:1, one launch (start us, length us, event | category | flops | bytes accessed | tf_op | source)
XLA Modules:
  0.0 62.2 jit_solution(11465874943279929376)
XLA Ops:
  0.0 0.0 copy-start
  0.0 0.0 copy-start.1
  0.0 59.2 %shard_map.82 = bf16[384,1024]{1,0:T(8,128)(2,1)} custom-call(bf16[384,1024]{1,0:T(8,128)(2,1)} %x_hbm.1, s32[1,384]{1,0:T(1,128)} %bitcast.7, bf16[1,1,128,2048]{3,2,1,0:T(8,128)(2,1)} %kv_hbm.1, s32[1,16]{1,0:T(1,128)} %mask_ref.1, f32[1,1024]{1,0:T(1,128)} %gin_ref.1, bf16[1,1024,2048]{2,1,0:T(8,128)(2,1)} %wuq_hbm.1, f32[1,1024]{1,0:T(1,128)} %gattn_ref.1), custom_call_target="tpu_custom_call" | custom-call | tf_op jit(solution)/shard_map/pallas_call | solution.py:356
  59.2 0.0 copy-done
  59.2 0.0 copy-done.1
  59.3 3.0 %add_convert_fusion = bf16[384,1024]{1,0:T(8,128)(2,1)} fusion(bf16[384,1024]{1,0:T(8,128)(2,1)S(1)} %copy-done.1, bf16[384,1024]{1,0:T(8,128)(2,1)} %shard_map.82, bf16[1,1024,1024]{2,1,0:T(8,128)(2,1)S(1)} %copy-done), kind=kOutput, calls=%fused_computation.2 | convolution fusion | flops 806486016 | bytes 4456448 | tf_op jit(solution)/shard_map/dot_general | solution.py:388
Async XLA Ops:
  0.0 59.2 %copy-start = (bf16[1,1024,1024]{2,1,0:T(8,128)(2,1)S(1)}, bf16[1,1024,1024]{2,1,0:T(8,128)(2,1)}, u32[]{:S(2)}) copy-start(bf16[1,1024,1024]{2,1,0:T(8,128)(2,1)} %param.15) | copy-start | bytes 6291460
  0.0 59.2 %copy-start.1 = (bf16[384,1024]{1,0:T(8,128)(2,1)S(1)}, bf16[384,1024]{1,0:T(8,128)(2,1)}, u32[]{:S(2)}) copy-start(bf16[384,1024]{1,0:T(8,128)(2,1)} %x_hbm.1) | copy-start | bytes 2359300

commit v5 on v4

--- a/solution.py
+++ b/solution.py
@@ -315,11 +315,7 @@
         pass_on(from_right, sibling, s_send, sl_recv.at[i])
         if i == 0:
             finish_first()
-        elif i < 6:
-            finish(i - 1)
-        if i == 5:
-            finish(5)
-    finish(6)
+        finish(i)
 
     for g, group in enumerate(GROUPS):
         exchange_wait(group, arecv, t_recv.at[g])

time: 62.4 us -> 61.2 us (0.981)
  Pallas kernels: 59.2 us -> 58.1 us
    pallas_call x1, Pallas kernels: 59.2 us -> 58.1 us  [on_device(): pl.pallas_call(kernel, out_shape=jax.ShapeDtypeStruct((ROWS, D), BF16), i...]
where the time goes in v5:
time: 61.2 us; the launch traced here: 61.1 us
  Pallas kernels  58.1 us (95%)
  matrix products  3 us (5%)
    pallas_call x1, Pallas kernels, on_device(): pl.pallas_call(kernel, out_shape=jax.ShapeDtypeStruct((ROWS, D), BF16), i...  58.1 us
    dot_general x1, matrix products, on_device(): scored = jnp.dot(mixed, w_out[0], preferred_element_type=F32)  3 us

profile of v5, /device:TPU:1, one launch (start us, length us, event | category | flops | bytes accessed | tf_op | source)
XLA Modules:
  0.0 61.1 jit_solution(4843494569047904909)
XLA Ops:
  0.0 0.0 copy-start
  0.0 0.0 copy-start.1
  0.0 58.1 %shard_map.82 = bf16[384,1024]{1,0:T(8,128)(2,1)} custom-call(bf16[384,1024]{1,0:T(8,128)(2,1)} %x_hbm.1, s32[1,384]{1,0:T(1,128)} %bitcast.7, bf16[1,1,128,2048]{3,2,1,0:T(8,128)(2,1)} %kv_hbm.1, s32[1,16]{1,0:T(1,128)} %mask_ref.1, f32[1,1024]{1,0:T(1,128)} %gin_ref.1, bf16[1,1024,2048]{2,1,0:T(8,128)(2,1)} %wuq_hbm.1, f32[1,1024]{1,0:T(1,128)} %gattn_ref.1), custom_call_target="tpu_custom_call" | custom-call | tf_op jit(solution)/shard_map/pallas_call | solution.py:352
  58.1 0.0 copy-done
  58.1 0.0 copy-done.1
  58.1 3.0 %add_convert_fusion = bf16[384,1024]{1,0:T(8,128)(2,1)} fusion(bf16[384,1024]{1,0:T(8,128)(2,1)S(1)} %copy-done.1, bf16[384,1024]{1,0:T(8,128)(2,1)} %shard_map.82, bf16[1,1024,1024]{2,1,0:T(8,128)(2,1)S(1)} %copy-done), kind=kOutput, calls=%fused_computation.2 | convolution fusion | flops 806486016 | bytes 4456448 | tf_op jit(solution)/shard_map/dot_general | solution.py:384
Async XLA Ops:
  0.0 58.1 %copy-start = (bf16[1,1024,1024]{2,1,0:T(8,128)(2,1)S(1)}, bf16[1,1024,1024]{2,1,0:T(8,128)(2,1)}, u32[]{:S(2)}) copy-start(bf16[1,1024,1024]{2,1,0:T(8,128)(2,1)} %param.15) | copy-start | bytes 6291460
  0.0 58.1 %copy-start.1 = (bf16[384,1024]{1,0:T(8,128)(2,1)S(1)}, bf16[384,1024]{1,0:T(8,128)(2,1)}, u32[]{:S(2)}) copy-start(bf16[384,1024]{1,0:T(8,128)(2,1)} %x_hbm.1) | copy-start | bytes 2359300

commit v6 on v5

--- a/solution.py
+++ b/solution.py
@@ -165,7 +165,7 @@
             ).start()
             return carry
 
-        lax.fori_loop(1, USERS, send, 0)
+        lax.fori_loop(1, USERS, send, 0, unroll=True)
         for order in group:
             target[order, slot_rows(me_u), :] = source[order, slot_rows(me_u), :]
 

time: 61.2 us -> 61.6 us (level)
  no operation moved by 1% of the time
where the time goes in v6:
time: 61.6 us; the launch traced here: 61.4 us
  Pallas kernels  58.4 us (95%)
  matrix products  2.99 us (5%)
    pallas_call x1, Pallas kernels, on_device(): pl.pallas_call(kernel, out_shape=jax.ShapeDtypeStruct((ROWS, D), BF16), i...  58.4 us
    dot_general x1, matrix products, on_device(): scored = jnp.dot(mixed, w_out[0], preferred_element_type=F32)  2.99 us

profile of v6, /device:TPU:1, one launch (start us, length us, event | category | flops | bytes accessed | tf_op | source)
XLA Modules:
  0.0 61.4 jit_solution(1202236064197381384)
XLA Ops:
  0.0 0.0 copy-start
  0.0 0.0 copy-start.1
  0.0 58.4 %shard_map.82 = bf16[384,1024]{1,0:T(8,128)(2,1)} custom-call(bf16[384,1024]{1,0:T(8,128)(2,1)} %x_hbm.1, s32[1,384]{1,0:T(1,128)} %bitcast.7, bf16[1,1,128,2048]{3,2,1,0:T(8,128)(2,1)} %kv_hbm.1, s32[1,16]{1,0:T(1,128)} %mask_ref.1, f32[1,1024]{1,0:T(1,128)} %gin_ref.1, bf16[1,1024,2048]{2,1,0:T(8,128)(2,1)} %wuq_hbm.1, f32[1,1024]{1,0:T(1,128)} %gattn_ref.1), custom_call_target="tpu_custom_call" | custom-call | tf_op jit(solution)/shard_map/pallas_call | solution.py:352
  58.4 0.0 copy-done
  58.4 0.0 copy-done.1
  58.4 3.0 %add_convert_fusion = bf16[384,1024]{1,0:T(8,128)(2,1)} fusion(bf16[384,1024]{1,0:T(8,128)(2,1)S(1)} %copy-done.1, bf16[384,1024]{1,0:T(8,128)(2,1)} %shard_map.82, bf16[1,1024,1024]{2,1,0:T(8,128)(2,1)S(1)} %copy-done), kind=kOutput, calls=%fused_computation.2 | convolution fusion | flops 806486016 | bytes 4456448 | tf_op jit(solution)/shard_map/dot_general | solution.py:384
Async XLA Ops:
  0.0 58.4 %copy-start = (bf16[1,1024,1024]{2,1,0:T(8,128)(2,1)S(1)}, bf16[1,1024,1024]{2,1,0:T(8,128)(2,1)}, u32[]{:S(2)}) copy-start(bf16[1,1024,1024]{2,1,0:T(8,128)(2,1)} %param.15) | copy-start | bytes 6291460
  0.0 58.4 %copy-start.1 = (bf16[384,1024]{1,0:T(8,128)(2,1)S(1)}, bf16[384,1024]{1,0:T(8,128)(2,1)}, u32[]{:S(2)}) copy-start(bf16[384,1024]{1,0:T(8,128)(2,1)} %x_hbm.1) | copy-start | bytes 2359300

commit v7 on v6

--- a/solution.py
+++ b/solution.py
@@ -77,13 +77,6 @@
             lsem.at[2 + half],
         )
 
-    load_x.start()
-    for order in range(H):
-        load_query_weight(order).start()
-    for half in range(2):
-        load_own(half).start()
-    load_wg.start()
-
     barrier = pltpu.get_barrier_semaphore()
 
     def greet(d, carry):
@@ -95,7 +88,9 @@
         )
         return carry
 
-    lax.fori_loop(1, 16, greet, 0)
+    lax.fori_loop(1, 16, greet, 0, unroll=True)
+    load_x.start()
+    load_query_weight(0).start()
     pl.semaphore_wait(barrier, 30)
 
     def send_blocks(half):
@@ -111,13 +106,18 @@
             ).start()
             return carry
 
-        lax.fori_loop(1, CTX, send, 0)
+        lax.fori_loop(1, CTX, send, 0, unroll=True)
 
     def blocks_wait(half, sem):
         got = landed[half].at[pl.ds(0, CTX - 1)]
         pltpu.make_async_copy(got, got, sem.at[half]).wait()
 
     send_blocks(0)
+    for order in range(1, H):
+        load_query_weight(order).start()
+    for half in range(2):
+        load_own(half).start()
+    load_wg.start()
 
     row_id = lax.broadcasted_iota(jnp.int32, (ROWS, ROWS), 0)
     col_id = lax.broadcasted_iota(jnp.int32, (ROWS, ROWS), 1)
@@ -293,9 +293,11 @@
         if opening:
             exchange_wait(GROUPS[s], qr, q_recv.at[s])
         (lo, lo_half), (hi, hi_half) = units_of(i)
-        arrived(piece(1 - core, head_at(lo), lo_half), sr_recv.at[i])
+        for sub in range(2):
+            arrived(quarter(piece(1 - core, head_at(lo), lo_half), sub), sr_recv.at[i, sub])
         attend(lo, lo_half, opening)
-        arrived(piece(1 - core, head_at(hi), hi_half), sl_recv.at[i])
+        for sub in range(2):
+            arrived(quarter(piece(1 - core, head_at(hi), hi_half), sub), sl_recv.at[i, sub])
         attend(hi, hi_half, opening and s < 4)
         if not opening or s == 4:
             send_attended(s)
@@ -308,11 +310,11 @@
             arrived(quarter(from_left, sub), r_recv.at[i, sub])
             if i < 5:
                 pass_on(quarter(from_left, sub), right, r_send, r_recv.at[i + 2, sub])
+            pass_on(quarter(from_left, sub), sibling, s_send, sr_recv.at[i, sub])
             arrived(quarter(from_right, sub), l_recv.at[i, sub])
             if i < 4 or i == 5:
                 pass_on(quarter(from_right, sub), left, l_send, l_recv.at[min(i + 2, 6), sub])
-        pass_on(from_left, sibling, s_send, sr_recv.at[i])
-        pass_on(from_right, sibling, s_send, sl_recv.at[i])
+            pass_on(quarter(from_right, sub), sibling, s_send, sl_recv.at[i, sub])
         if i == 0:
             finish_first()
         finish(i)
@@ -375,7 +377,7 @@
             pltpu.VMEM((SLOTS, ROWS), BF16),
             pltpu.VMEM((ROWS, SLOTS), BF16),
             dma((4,)), dma((H,)), dma((2,)), dma((2,)), dma((5,)), dma((5,)), dma((5,)), dma((5,)),
-            dma(()), dma(()), dma(()), dma((7, 2)), dma((7, 2)), dma((2,)), dma((7,)), dma((7,)),
+            dma(()), dma(()), dma(()), dma((7, 2)), dma((7, 2)), dma((2,)), dma((7, 2)), dma((7, 2)),
         ],
         compiler_params=pltpu.CompilerParams(
             collective_id=0, has_side_effects=True, vmem_limit_bytes=56 * 1024 * 1024

time: 61.6 us -> 61.3 us (level)
  no operation moved by 1% of the time
where the time goes in v7:
time: 61.3 us; the launch traced here: 61.2 us
  Pallas kernels  58.2 us (95%)
  matrix products  3 us (5%)
    pallas_call x1, Pallas kernels, on_device(): pl.pallas_call(kernel, out_shape=jax.ShapeDtypeStruct((ROWS, D), BF16), i...  58.2 us
    dot_general x1, matrix products, on_device(): scored = jnp.dot(mixed, w_out[0], preferred_element_type=F32)  3 us

profile of v7, /device:TPU:1, one launch (start us, length us, event | category | flops | bytes accessed | tf_op | source)
XLA Modules:
  0.0 61.2 jit_solution(548381158958829740)
XLA Ops:
  0.0 0.0 copy-start
  0.0 0.0 copy-start.1
  0.0 58.2 %shard_map.82 = bf16[384,1024]{1,0:T(8,128)(2,1)} custom-call(bf16[384,1024]{1,0:T(8,128)(2,1)} %x_hbm.1, s32[1,384]{1,0:T(1,128)} %bitcast.7, bf16[1,1,128,2048]{3,2,1,0:T(8,128)(2,1)} %kv_hbm.1, s32[1,16]{1,0:T(1,128)} %mask_ref.1, f32[1,1024]{1,0:T(1,128)} %gin_ref.1, bf16[1,1024,2048]{2,1,0:T(8,128)(2,1)} %wuq_hbm.1, f32[1,1024]{1,0:T(1,128)} %gattn_ref.1), custom_call_target="tpu_custom_call" | custom-call | tf_op jit(solution)/shard_map/pallas_call | solution.py:354
  58.2 0.0 copy-done
  58.2 0.0 copy-done.1
  58.2 3.0 %add_convert_fusion = bf16[384,1024]{1,0:T(8,128)(2,1)} fusion(bf16[384,1024]{1,0:T(8,128)(2,1)S(1)} %copy-done.1, bf16[384,1024]{1,0:T(8,128)(2,1)} %shard_map.82, bf16[1,1024,1024]{2,1,0:T(8,128)(2,1)S(1)} %copy-done), kind=kOutput, calls=%fused_computation.2 | convolution fusion | flops 806486016 | bytes 4456448 | tf_op jit(solution)/shard_map/dot_general | solution.py:386
Async XLA Ops:
  0.0 58.2 %copy-start = (bf16[1,1024,1024]{2,1,0:T(8,128)(2,1)S(1)}, bf16[1,1024,1024]{2,1,0:T(8,128)(2,1)}, u32[]{:S(2)}) copy-start(bf16[1,1024,1024]{2,1,0:T(8,128)(2,1)} %param.15) | copy-start | bytes 6291460
  0.0 58.2 %copy-start.1 = (bf16[384,1024]{1,0:T(8,128)(2,1)S(1)}, bf16[384,1024]{1,0:T(8,128)(2,1)}, u32[]{:S(2)}) copy-start(bf16[384,1024]{1,0:T(8,128)(2,1)} %x_hbm.1) | copy-start | bytes 2359300
